TPU v7x, 32 devices: a whole 2x2x4 slice. The times are simulated.
32 devices in a mesh: basin: 2 (over x), pair: 8 (over z, y), row: 2 (over core).
Axes of the slice: x: 2, y: 2, z: 4, core: 2. Of those that a mesh axis runs over, the one named last changes fastest.
Arguments:
- snapshots: float32 [8192, 4096], P(('basin', 'row'), 'pair'), parts along dimension 0, may hold values from -60 to 60, as said below
- plan: int32 [4, 16], replicated, may hold values from 0 to 15, as said below
Outputs:
- rotated: float32 [8192, 4096], P(('basin', 'row'), 'pair'), parts along dimension 0
There are 2 independent parts, one for each index of `basin`. A program takes and returns all parts, laid end to end along the dimension named above; an argument that names none is the same for every part. Nothing has to cross between parts.
Inputs may be any that keep to these rules, and one draw needn't show every extreme that they name: `plan`: each row of the table is a permutation of the 16 slots. Slots 2d and 2d + 1 lie on the d-th index of pair; in every round each index sends one of its two blocks to index d + 1 and the other to index d - 1 (both modulo 8). `snapshots`: real values.
All inputs are finite; a program needn't handle non-finite values.
Results may differ from a plain program's by a relative error of at most 0.0003.
Values sent between devices are 32-bit elements; how exact they have to be, the bound alone decides.
A program may use at most 64 MiB of HBM per device.

v0:
```python
import jax
import jax.numpy as jnp
from jax import lax
from jax.sharding import PartitionSpec as P

NS_ITERS = 6
epsilon = 1e-06


def from_behind(value, axis, by):
    size = lax.axis_size(axis)
    return lax.ppermute(value, axis, [(i, (i + by) % size) for i in range(size)])


def matmul(left, right):
    return jnp.dot(left, right, precision=lax.Precision.HIGHEST, preferred_element_type=jnp.float32)


def contract(left, right, left_dim, right_dim):
    return lax.dot_general(
        left,
        right,
        (((left_dim,), (right_dim,)), ((), ())),
        precision=lax.Precision.HIGHEST,
        preferred_element_type=jnp.float32,
    )


def per_device(snapshots, plan):
    width = snapshots.shape[1] // 2
    first_block = snapshots[:, :width]
    second_block = snapshots[:, width:]
    device = lax.axis_index("pair")
    pair_count = lax.axis_size("pair")
    below = (device + pair_count - 1) % pair_count
    above = (device + 1) % pair_count
    identity = jnp.eye(width, dtype=jnp.float32)
    for round_index in range(plan.shape[0]):
        joined = jnp.concatenate((first_block, second_block), axis=1)
        total = lax.psum(contract(joined, joined, 0, 0), "row")
        cross = total[:width, width:]
        diagonal = jnp.diagonal(total)
        norm_first = diagonal[:width]
        norm_second = diagonal[width:]
        coupling = cross / (norm_first[:, None] + norm_second[None, :] + epsilon)
        system = identity + contract(coupling, coupling, 1, 1)
        inverse = identity / (1.0 + jnp.sum(coupling * coupling))
        for sweep in range(NS_ITERS):
            inverse = matmul(inverse, 2.0 * identity - matmul(system, inverse))
        lifted = first_block - contract(second_block, coupling, 1, 1)
        mixed = matmul(lifted, inverse)
        new_first = 2.0 * mixed - first_block
        new_second = second_block + 2.0 * matmul(mixed, coupling)
        layout = plan[round_index]
        upper_zero = lax.dynamic_index_in_dim(layout, 2 * above, 0, False)
        upper_one = lax.dynamic_index_in_dim(layout, 2 * above + 1, 0, False)
        second_goes_up = (upper_zero == 2 * device + 1) | (upper_one == 2 * device + 1)
        going_up = jnp.where(second_goes_up, new_second, new_first)
        going_down = jnp.where(second_goes_up, new_first, new_second)
        from_below = from_behind(going_up, "pair", 1)
        from_above = from_behind(going_down, "pair", -1)
        source_zero = lax.dynamic_index_in_dim(layout, 2 * device, 0, False)
        zero_from_below = source_zero // 2 == below
        first_block = jnp.where(zero_from_below, from_below, from_above)
        second_block = jnp.where(zero_from_below, from_above, from_below)
    return jnp.concatenate((first_block, second_block), axis=1)


def solution(mesh):
    in_specs = (P(("basin", "row"), "pair"), P())
    out_specs = P(("basin", "row"), "pair")
    return jax.shard_map(
        per_device, mesh=mesh, in_specs=in_specs, out_specs=out_specs, check_vma=False
    )
```

profile of v0, /device:TPU:0, one launch (start us, length us, event | category | flops | bytes accessed | tf_op | source)
XLA Modules:
  0.0 619.5 jit_solution(1463069651718162065)
XLA Ops:
  6.5 11.1 %fusion.62 = f32[512,512]{1,0:T(8,128)} fusion(f32[2048,512]{1,0:T(8,128)} %param.2), kind=kOutput, calls=%fused_computation.145 | convolution fusion | flops 6442450944 | bytes 5242880 | tf_op jit(solution)/shard_map/dot_general | solution.py:20
  20.0 20.1 %all-reduce.5.cloned.1.call-done = f32[512,512]{1,0:T(8,128)} async-done(((f32[512,512]{1,0:T(8,128)}), f32[512,512]{1,0:T(8,128)}) %all-reduce.5.cloned.1.call-update) | async-done | bytes 1048592 | tf_op jit(solution)/shard_map/psum | solution.py:40
  40.1 8.6 %gather_fusion = f32[512]{0:T(512)S(1)} fusion(f32[512,512]{1,0:T(8,128)} %all-reduce.5.cloned.1.call-done, s32[512]{0:T(512)S(1)} %bitcast.122), kind=kCustom, calls=%fused_computation | custom fusion | bytes 8192 | tf_op jit(solution)/shard_map/jit(diagonal)/cond/branch_0_fun/gather | solution.py:42
  55.3 2.1 fusion.16
  59.3 3.6 broadcast_select_fusion
  64.6 3.5 collective-permute-start
  70.6 84.6 %collective-permute-done.1 = f32[2048,256]{1,0:T(8,128)} collective-permute-done((f32[2048,256]{1,0:T(8,128)}, f32[2048,256]{1,0:T(8,128)}, u32[]{:S(2)}, u32[]{:S(2)}) %collective-permute-start.1) | collective-permute-done | bytes 2097184 | tf_op jit(solution)/shard_map/ppermute | solution.py:12
  155.2 2.5 collective-permute-done
  157.7 2.5 broadcast_select_fusion.2
  161.5 8.0 %fusion = f32[512,512]{1,0:T(8,128)} fusion(f32[2048,256]{1,0:T(8,128)S(1)} %get-tuple-element.20, f32[2048,256]{1,0:T(8,128)S(1)} %get-tuple-element.19), kind=kOutput, calls=%fused_computation.4 | convolution fusion | flops 6443499520 | bytes 5242880 | tf_op jit(solution)/shard_map/dot_general | solution.py:20
  171.0 17.7 %all-reduce.7.cloned.1.call-done = f32[512,512]{1,0:T(8,128)} async-done(((f32[512,512]{1,0:T(8,128)}), f32[512,512]{1,0:T(8,128)}) %all-reduce.7.cloned.1.call-update) | async-done | bytes 1048592 | tf_op jit(solution)/shard_map/psum | solution.py:40
  188.7 8.6 %gather_fusion.1 = f32[512]{0:T(512)S(1)} fusion(f32[512,512]{1,0:T(8,128)} %all-reduce.7.cloned.1.call-done, s32[512]{0:T(512)S(1)} %bitcast.123), kind=kCustom, calls=%fused_computation.1 | custom fusion | bytes 8192 | tf_op jit(solution)/shard_map/jit(diagonal)/cond/branch_0_fun/gather | solution.py:42
  207.9 4.4 broadcast_select_fusion.5
  214.0 3.2 collective-permute-start.3
  219.7 84.9 %collective-permute-done.2 = f32[2048,256]{1,0:T(8,128)S(1)} collective-permute-done((f32[2048,256]{1,0:T(8,128)}, f32[2048,256]{1,0:T(8,128)S(1)}, u32[]{:S(2)}, u32[]{:S(2)}) %collective-permute-start.2) | collective-permute-done | bytes 2097184 | tf_op jit(solution)/shard_map/ppermute | solution.py:12
  307.0 2.5 broadcast_select_fusion.7
  310.8 8.0 %fusion.4 = f32[512,512]{1,0:T(8,128)} fusion(f32[2048,256]{1,0:T(8,128)S(1)} %get-tuple-element.18, f32[2048,256]{1,0:T(8,128)S(1)} %get-tuple-element.17), kind=kOutput, calls=%fused_computation.8 | convolution fusion | flops 6443499520 | bytes 5242880 | tf_op jit(solution)/shard_map/dot_general | solution.py:20
  321.3 18.1 %all-reduce.9.cloned.1.call-done = f32[512,512]{1,0:T(8,128)} async-done(((f32[512,512]{1,0:T(8,128)}), f32[512,512]{1,0:T(8,128)}) %all-reduce.9.cloned.1.call-update) | async-done | bytes 1048592 | tf_op jit(solution)/shard_map/psum | solution.py:40
  339.4 8.6 %gather_fusion.2 = f32[512]{0:T(512)S(1)} fusion(f32[512,512]{1,0:T(8,128)} %all-reduce.9.cloned.1.call-done, s32[512]{0:T(512)S(1)} %bitcast.124), kind=kCustom, calls=%fused_computation.2 | custom fusion | bytes 8192 | tf_op jit(solution)/shard_map/jit(diagonal)/cond/branch_0_fun/gather | solution.py:42
  358.5 4.4 broadcast_select_fusion.8
  364.7 3.1 collective-permute-start.4
  370.3 84.9 %collective-permute-done.5 = f32[2048,256]{1,0:T(8,128)S(1)} collective-permute-done((f32[2048,256]{1,0:T(8,128)}, f32[2048,256]{1,0:T(8,128)S(1)}, u32[]{:S(2)}, u32[]{:S(2)}) %collective-permute-start.5) | collective-permute-done | bytes 2097184 | tf_op jit(solution)/shard_map/ppermute | solution.py:12
  457.6 2.5 broadcast_select_fusion.10
  461.4 8.0 %fusion.8 = f32[512,512]{1,0:T(8,128)} fusion(f32[2048,256]{1,0:T(8,128)S(1)} %get-tuple-element.16, f32[2048,256]{1,0:T(8,128)S(1)} %get-tuple-element.15), kind=kOutput, calls=%fused_computation.12 | convolution fusion | flops 6443499520 | bytes 5242880 | tf_op jit(solution)/shard_map/dot_general | solution.py:20
  470.7 19.3 %all-reduce.11.cloned.1.call-done = f32[512,512]{1,0:T(8,128)} async-done(((f32[512,512]{1,0:T(8,128)}), f32[512,512]{1,0:T(8,128)}) %all-reduce.11.cloned.1.call-update) | async-done | bytes 1048592 | tf_op jit(solution)/shard_map/psum | solution.py:40
  490.0 8.8 %gather_fusion.3 = f32[512]{0:T(512)S(1)} fusion(f32[512,512]{1,0:T(8,128)} %all-reduce.11.cloned.1.call-done, s32[512]{0:T(512)S(1)} %bitcast.125), kind=kCustom, calls=%fused_computation.3 | custom fusion | bytes 8192 | tf_op jit(solution)/shard_map/jit(diagonal)/cond/branch_0_fun/gather | solution.py:42
  505.5 2.0 convolution_subtract_fusion
  509.4 4.4 broadcast_select_fusion.13
  515.5 3.0 collective-permute-start.7
  521.0 85.1 %collective-permute-done.6 = f32[2048,256]{1,0:T(8,128)S(1)} collective-permute-done((f32[2048,256]{1,0:T(8,128)}, f32[2048,256]{1,0:T(8,128)S(1)}, u32[]{:S(2)}, u32[]{:S(2)}) %collective-permute-start.6) | collective-permute-done | bytes 2097184 | tf_op jit(solution)/shard_map/ppermute | solution.py:12
  606.1 2.2 collective-permute-done.7
  610.1 2.5 pad_maximum_fusion
  (113 shorter events, 54.9 us)
Async XLA Ops:
  6.5 11.5 %copy-start.13 = (s32[4,16]{1,0:T(4,128)S(1)}, s32[4,16]{1,0:T(4,128)}, u32[]{:S(2)}) copy-start(s32[4,16]{1,0:T(4,128)} %param.3) | copy-start | bytes 772
  6.5 33.6 %all-reduce.5.cloned.1.call-start = ((), (), s32[]{:S(2)}) async-start(), calls=%async_computation | async-start | bytes 2097152 | tf_op jit(solution)/shard_map/psum | solution.py:40
  17.7 171.1 %all-reduce.7.cloned.1.call-start = ((), (), s32[]{:S(2)}) async-start(), calls=%async_computation.1 | async-start | bytes 2097152 | tf_op jit(solution)/shard_map/psum | solution.py:40
  40.1 8.6 %copy-start.7 = (f32[512,512]{1,0:T(8,128)S(1)}, f32[512,512]{1,0:T(8,128)}, u32[]{:S(2)}) copy-start(f32[512,512]{1,0:T(8,128)} %all-reduce.5.cloned.1.call-done) | copy-start | bytes 3145732
  53.0 2.3 copy-start
  62.9 92.3 %collective-permute-start.1 = (f32[2048,256]{1,0:T(8,128)}, f32[2048,256]{1,0:T(8,128)}, u32[]{:S(2)}, u32[]{:S(2)}) collective-permute-start(f32[2048,256]{1,0:T(8,128)} %get-tuple-element.5), channel_id=1, source_target_pairs={{0,2},{2,4},{4,6},{6,8},{8,10},{10,12},{12,14},{14,0},{1,3},{3,5},... | collective-permute-start | bytes 6291464 | tf_op jit(solution)/shard_map/ppermute | solution.py:12
  64.6 93.1 %collective-permute-start = (f32[2048,256]{1,0:T(8,128)S(1)}, f32[2048,256]{1,0:T(8,128)}, u32[]{:S(2)}, u32[]{:S(2)}) collective-permute-start(f32[2048,256]{1,0:T(8,128)S(1)} %get-tuple-element.6), channel_id=1, source_target_pairs={{0,14},{2,0},{4,2},{6,4},{8,6},{10,8},{12,10},{14,12},{1,15},{3,1}... | collective-permute-start | bytes 6291464 | tf_op jit(solution)/shard_map/ppermute | solution.py:12
  160.2 1.3 copy-start.5
  169.5 169.8 %all-reduce.9.cloned.1.call-start = ((), (), s32[]{:S(2)}) async-start(), calls=%async_computation.2 | async-start | bytes 2097152 | tf_op jit(solution)/shard_map/psum | solution.py:40
  188.7 8.6 %copy-start.10 = (f32[512,512]{1,0:T(8,128)S(1)}, f32[512,512]{1,0:T(8,128)}, u32[]{:S(2)}) copy-start(f32[512,512]{1,0:T(8,128)} %all-reduce.7.cloned.1.call-done) | copy-start | bytes 3145732
  202.1 1.9 copy-start.6
  212.3 92.3 %collective-permute-start.2 = (f32[2048,256]{1,0:T(8,128)}, f32[2048,256]{1,0:T(8,128)S(1)}, u32[]{:S(2)}, u32[]{:S(2)}) collective-permute-start(f32[2048,256]{1,0:T(8,128)} %get-tuple-element.11), channel_id=1, source_target_pairs={{0,2},{2,4},{4,6},{6,8},{8,10},{10,12},{12,14},{14,0},{1,3},{3,5},... | collective-permute-start | bytes 6291464 | tf_op jit(solution)/shard_map/ppermute | solution.py:12
  214.0 93.0 %collective-permute-start.3 = (f32[2048,256]{1,0:T(8,128)}, f32[2048,256]{1,0:T(8,128)}, u32[]{:S(2)}, u32[]{:S(2)}) collective-permute-start(f32[2048,256]{1,0:T(8,128)} %get-tuple-element.12), channel_id=1, source_target_pairs={{0,14},{2,0},{4,2},{6,4},{8,6},{10,8},{12,10},{14,12},{1,15},{3,1}... | collective-permute-start | bytes 6291464 | tf_op jit(solution)/shard_map/ppermute | solution.py:12
  304.6 1.3 copy-start.11
  309.5 1.3 copy-start.1
  318.9 171.1 %all-reduce.11.cloned.1.call-start = ((), (), s32[]{:S(2)}) async-start(), calls=%async_computation.3 | async-start | bytes 2097152 | tf_op jit(solution)/shard_map/psum | solution.py:40
  339.3 8.6 %copy-start.8 = (f32[512,512]{1,0:T(8,128)S(1)}, f32[512,512]{1,0:T(8,128)}, u32[]{:S(2)}) copy-start(f32[512,512]{1,0:T(8,128)} %all-reduce.9.cloned.1.call-done) | copy-start | bytes 3145732
  352.7 1.9 copy-start.2
  362.9 92.3 %collective-permute-start.5 = (f32[2048,256]{1,0:T(8,128)}, f32[2048,256]{1,0:T(8,128)S(1)}, u32[]{:S(2)}, u32[]{:S(2)}) collective-permute-start(f32[2048,256]{1,0:T(8,128)} %get-tuple-element.9), channel_id=1, source_target_pairs={{0,2},{2,4},{4,6},{6,8},{8,10},{10,12},{12,14},{14,0},{1,3},{3,5},... | collective-permute-start | bytes 6291464 | tf_op jit(solution)/shard_map/ppermute | solution.py:12
  364.7 92.9 %collective-permute-start.4 = (f32[2048,256]{1,0:T(8,128)}, f32[2048,256]{1,0:T(8,128)}, u32[]{:S(2)}, u32[]{:S(2)}) collective-permute-start(f32[2048,256]{1,0:T(8,128)} %get-tuple-element.10), channel_id=1, source_target_pairs={{0,14},{2,0},{4,2},{6,4},{8,6},{10,8},{12,10},{14,12},{1,15},{3,1}... | collective-permute-start | bytes 6291464 | tf_op jit(solution)/shard_map/ppermute | solution.py:12
  455.2 1.3 copy-start.12
  460.1 1.3 copy-start.3
  490.0 8.8 %copy-start.9 = (f32[512,512]{1,0:T(8,128)S(1)}, f32[512,512]{1,0:T(8,128)}, u32[]{:S(2)}) copy-start(f32[512,512]{1,0:T(8,128)} %all-reduce.11.cloned.1.call-done) | copy-start | bytes 3145732
  503.6 1.9 copy-start.4
  513.7 92.3 %collective-permute-start.6 = (f32[2048,256]{1,0:T(8,128)}, f32[2048,256]{1,0:T(8,128)S(1)}, u32[]{:S(2)}, u32[]{:S(2)}) collective-permute-start(f32[2048,256]{1,0:T(8,128)} %get-tuple-element.7), channel_id=1, source_target_pairs={{0,2},{2,4},{4,6},{6,8},{8,10},{10,12},{12,14},{14,0},{1,3},{3,5},... | collective-permute-start | bytes 6291464 | tf_op jit(solution)/shard_map/ppermute | solution.py:12
  515.5 92.8 %collective-permute-start.7 = (f32[2048,256]{1,0:T(8,128)}, f32[2048,256]{1,0:T(8,128)}, u32[]{:S(2)}, u32[]{:S(2)}) collective-permute-start(f32[2048,256]{1,0:T(8,128)} %get-tuple-element.8), channel_id=1, source_target_pairs={{0,14},{2,0},{4,2},{6,4},{8,6},{10,8},{12,10},{14,12},{1,15},{3,1}... | collective-permute-start | bytes 6291464 | tf_op jit(solution)/shard_map/ppermute | solution.py:12
Sparse Core Ops, SparseCore 0:
  17.8 22.2 all-reduce.4
  169.7 19.0 all-reduce.6
  319.0 20.3 all-reduce.8
  469.6 20.3 all-reduce.10
where the time goes:
time: 624 us; the launch traced here: 619 us
  waiting for transfers between devices  422 us (68%)
  matrix products  87.4 us (14%)
  local copies, waits for them, and re-layouts  42.5 us (7%)
  between operations  32.2 us (5%)
  starting transfers between devices  20.7 us (3%)
  other arithmetic  15.1 us (2%)
    ppermute x8, waiting for transfers between devices, from_behind(): lax.ppermute(value, axis, [(i, (i + by) % size) for i in range(size)])  346 us
    psum x4, waiting for transfers between devices, per_device(): total = lax.psum(contract(joined, joined, 0, 0), 'row')  75.2 us
    dot_general x12, matrix products, contract(): lax.dot_general(left, right, (((left_dim,), (right_dim,)), ((), ())), pre...  45.1 us
    dot_general x56, matrix products, matmul(): jnp.dot(left, right, precision=lax.Precision.HIGHEST, preferred_element_t...  42.3 us
    gather x4, local copies, waits for them, and re-layouts, per_device(): diagonal = jnp.diagonal(total)  34.5 us
    ppermute x8, starting transfers between devices, from_behind(): lax.ppermute(value, axis, [(i, (i + by) % size) for i in range(size)])  19.7 us
  transfers between devices with their start and end apart: 12, of which 12 were waited for; matrix products, arithmetic and copies ran while one was open for 0% of the time, Pallas kernels for 0%

commit v1 on v0

--- a/solution.py
+++ b/solution.py
@@ -37,7 +37,7 @@
     identity = jnp.eye(width, dtype=jnp.float32)
     for round_index in range(plan.shape[0]):
         joined = jnp.concatenate((first_block, second_block), axis=1)
-        total = lax.psum(contract(joined, joined, 0, 0), "row")
+        total = jnp.sum(lax.all_gather(contract(joined, joined, 0, 0), "row"), axis=0)
         cross = total[:width, width:]
         diagonal = jnp.diagonal(total)
         norm_first = diagonal[:width]

time: 624 us -> 590 us (0.946)
  waiting for transfers between devices: 422 us -> 385 us
  local copies, waits for them, and re-layouts: 42.5 us -> 26.6 us
  matrix products: 87.4 us -> 98.4 us
  other arithmetic: 15.1 us -> 22.9 us
    psum x4 -> x0, waiting for transfers between devices: 75.2 us -> none  [per_device(): total = lax.psum(contract(joined, joined, 0, 0), 'row')]
    all_gather x0 -> x4, waiting for transfers between devices: none -> 39.2 us  [per_device(): lax.all_gather(contract(joined, joined, 0, 0), 'row')]
    gather x4, local copies, waits for them, and re-layouts: 34.5 us -> 18.3 us  [per_device(): diagonal = jnp.diagonal(total)]
    dot_general x12, matrix products: 45.1 us -> 56.1 us  [contract(): lax.dot_general(left, right, (((left_dim,), (right_dim,)), ((), ())), pre...]
    reduce_sum x0 -> x4, other arithmetic: none -> 7.75 us  [per_device(): jnp.sum(lax.all_gather(contract(joined, joined, 0, 0), 'row'), axis=0)]
where the time goes in v1:
time: 590 us; the launch traced here: 586 us
  waiting for transfers between devices  385 us (65%)
  matrix products  98.4 us (17%)
  between operations  32.5 us (6%)
  local copies, waits for them, and re-layouts  26.6 us (5%)
  other arithmetic  22.9 us (4%)
  starting transfers between devices  20.8 us (4%)
    ppermute x8, waiting for transfers between devices, from_behind(): lax.ppermute(value, axis, [(i, (i + by) % size) for i in range(size)])  346 us
    dot_general x12, matrix products, contract(): lax.dot_general(left, right, (((left_dim,), (right_dim,)), ((), ())), pre...  56.1 us
    dot_general x56, matrix products, matmul(): jnp.dot(left, right, precision=lax.Precision.HIGHEST, preferred_element_t...  42.3 us
    all_gather x4, waiting for transfers between devices, per_device(): lax.all_gather(contract(joined, joined, 0, 0), 'row')  39.2 us
    ppermute x8, starting transfers between devices, from_behind(): lax.ppermute(value, axis, [(i, (i + by) % size) for i in range(size)])  19.8 us
    gather x4, local copies, waits for them, and re-layouts, per_device(): diagonal = jnp.diagonal(total)  18.3 us
  transfers between devices with their start and end apart: 12, of which 12 were waited for; matrix products, arithmetic and copies ran while one was open for 0% of the time, Pallas kernels for 0%

profile of v1, /device:TPU:0, one launch (start us, length us, event | category | flops | bytes accessed | tf_op | source)
XLA Modules:
  0.0 586.3 jit_solution(6188238909545415348)
XLA Ops:
  6.5 11.1 %fusion.62 = f32[512,512]{1,0:T(8,128)} fusion(f32[2048,512]{1,0:T(8,128)} %param.2), kind=kOutput, calls=%fused_computation.145 | convolution fusion | flops 6442450944 | bytes 5242880 | tf_op jit(solution)/shard_map/dot_general | solution.py:20
  20.1 11.0 %all-gather.9.cloned.1.call-done = f32[1024,512]{1,0:T(8,128)} async-done(((f32[512,512]{1,0:T(8,128)}), f32[1024,512]{1,0:T(8,128)}) %all-gather.9.cloned.1.call-update) | async-done | bytes 2097168 | tf_op jit(solution)/shard_map/all_gather | solution.py:40
  33.0 4.5 gather_fusion
  38.8 4.3 fusion.16
  50.7 3.6 broadcast_select_fusion
  56.0 3.5 collective-permute-start
  62.1 84.5 %collective-permute-done.1 = f32[2048,256]{1,0:T(8,128)} collective-permute-done((f32[2048,256]{1,0:T(8,128)}, f32[2048,256]{1,0:T(8,128)}, u32[]{:S(2)}, u32[]{:S(2)}) %collective-permute-start.1) | collective-permute-done | bytes 2097184 | tf_op jit(solution)/shard_map/ppermute | solution.py:12
  146.6 2.5 collective-permute-done
  149.1 2.5 broadcast_select_fusion.2
  152.9 8.0 %fusion = f32[512,512]{1,0:T(8,128)} fusion(f32[2048,256]{1,0:T(8,128)S(1)} %get-tuple-element.20, f32[2048,256]{1,0:T(8,128)S(1)} %get-tuple-element.19), kind=kOutput, calls=%fused_computation.4 | convolution fusion | flops 6443499520 | bytes 5242880 | tf_op jit(solution)/shard_map/dot_general | solution.py:20
  162.4 8.7 %all-gather.11.cloned.1.call-done = f32[1024,512]{1,0:T(8,128)} async-done(((f32[512,512]{1,0:T(8,128)}), f32[1024,512]{1,0:T(8,128)}) %all-gather.11.cloned.1.call-update) | async-done | bytes 2097168 | tf_op jit(solution)/shard_map/all_gather | solution.py:40
  173.1 4.5 gather_fusion.1
  178.9 4.9 convolution_subtract_fusion.2
  191.1 4.4 broadcast_select_fusion.5
  197.2 3.2 collective-permute-start.3
  203.1 84.7 %collective-permute-done.2 = f32[2048,256]{1,0:T(8,128)S(1)} collective-permute-done((f32[2048,256]{1,0:T(8,128)}, f32[2048,256]{1,0:T(8,128)S(1)}, u32[]{:S(2)}, u32[]{:S(2)}) %collective-permute-start.2) | collective-permute-done | bytes 2097184 | tf_op jit(solution)/shard_map/ppermute | solution.py:12
  290.2 2.5 broadcast_select_fusion.7
  294.0 8.0 %fusion.4 = f32[512,512]{1,0:T(8,128)} fusion(f32[2048,256]{1,0:T(8,128)S(1)} %get-tuple-element.18, f32[2048,256]{1,0:T(8,128)S(1)} %get-tuple-element.17), kind=kOutput, calls=%fused_computation.8 | convolution fusion | flops 6443499520 | bytes 5242880 | tf_op jit(solution)/shard_map/dot_general | solution.py:20
  304.3 9.2 %all-gather.13.cloned.1.call-done = f32[1024,512]{1,0:T(8,128)} async-done(((f32[512,512]{1,0:T(8,128)}), f32[1024,512]{1,0:T(8,128)}) %all-gather.13.cloned.1.call-update) | async-done | bytes 2097168 | tf_op jit(solution)/shard_map/all_gather | solution.py:40
  315.5 4.5 gather_fusion.2
  321.4 4.9 convolution_subtract_fusion.1
  333.6 4.4 broadcast_select_fusion.8
  339.7 3.1 collective-permute-start.4
  345.4 84.9 %collective-permute-done.5 = f32[2048,256]{1,0:T(8,128)S(1)} collective-permute-done((f32[2048,256]{1,0:T(8,128)}, f32[2048,256]{1,0:T(8,128)S(1)}, u32[]{:S(2)}, u32[]{:S(2)}) %collective-permute-start.5) | collective-permute-done | bytes 2097184 | tf_op jit(solution)/shard_map/ppermute | solution.py:12
  436.4 8.0 %fusion.8 = f32[512,512]{1,0:T(8,128)} fusion(f32[2048,256]{1,0:T(8,128)S(1)} %get-tuple-element.16, f32[2048,256]{1,0:T(8,128)S(1)} %get-tuple-element.15), kind=kOutput, calls=%fused_computation.12 | convolution fusion | flops 6443499520 | bytes 5242880 | tf_op jit(solution)/shard_map/dot_general | solution.py:20
  445.7 10.3 %all-gather.15.cloned.1.call-done = f32[1024,512]{1,0:T(8,128)} async-done(((f32[512,512]{1,0:T(8,128)}), f32[1024,512]{1,0:T(8,128)}) %all-gather.15.cloned.1.call-update) | async-done | bytes 2097168 | tf_op jit(solution)/shard_map/all_gather | solution.py:40
  458.0 4.7 gather_fusion.3
  464.1 4.9 convolution_subtract_fusion
  476.2 4.4 broadcast_select_fusion.13
  482.3 3.0 collective-permute-start.7
  488.0 84.9 %collective-permute-done.6 = f32[2048,256]{1,0:T(8,128)S(1)} collective-permute-done((f32[2048,256]{1,0:T(8,128)}, f32[2048,256]{1,0:T(8,128)S(1)}, u32[]{:S(2)}, u32[]{:S(2)}) %collective-permute-start.6) | collective-permute-done | bytes 2097184 | tf_op jit(solution)/shard_map/ppermute | solution.py:12
  577.0 2.5 pad_maximum_fusion
  (115 shorter events, 63.6 us)
Async XLA Ops:
  6.5 11.5 %copy-start.12 = (s32[4,16]{1,0:T(4,128)S(1)}, s32[4,16]{1,0:T(4,128)}, u32[]{:S(2)}) copy-start(s32[4,16]{1,0:T(4,128)} %param.3) | copy-start | bytes 772
  6.5 24.5 %all-gather.9.cloned.1.call-start = ((), (), s32[]{:S(2)}) async-start(), calls=%async_computation | async-start | bytes 3145728 | tf_op jit(solution)/shard_map/all_gather | solution.py:40
  17.7 153.5 %all-gather.11.cloned.1.call-start = ((), (), s32[]{:S(2)}) async-start(), calls=%async_computation.1 | async-start | bytes 3145728 | tf_op jit(solution)/shard_map/all_gather | solution.py:40
  48.5 2.2 copy-start
  54.2 92.3 %collective-permute-start.1 = (f32[2048,256]{1,0:T(8,128)}, f32[2048,256]{1,0:T(8,128)}, u32[]{:S(2)}, u32[]{:S(2)}) collective-permute-start(f32[2048,256]{1,0:T(8,128)} %get-tuple-element.5), channel_id=1, source_target_pairs={{0,2},{2,4},{4,6},{6,8},{8,10},{10,12},{12,14},{14,0},{1,3},{3,5},... | collective-permute-start | bytes 6291464 | tf_op jit(solution)/shard_map/ppermute | solution.py:12
  56.0 93.1 %collective-permute-start = (f32[2048,256]{1,0:T(8,128)S(1)}, f32[2048,256]{1,0:T(8,128)}, u32[]{:S(2)}, u32[]{:S(2)}) collective-permute-start(f32[2048,256]{1,0:T(8,128)S(1)} %get-tuple-element.6), channel_id=1, source_target_pairs={{0,14},{2,0},{4,2},{6,4},{8,6},{10,8},{12,10},{14,12},{1,15},{3,1}... | collective-permute-start | bytes 6291464 | tf_op jit(solution)/shard_map/ppermute | solution.py:12
  151.6 1.3 copy-start.5
  161.0 152.6 %all-gather.13.cloned.1.call-start = ((), (), s32[]{:S(2)}) async-start(), calls=%async_computation.2 | async-start | bytes 3145728 | tf_op jit(solution)/shard_map/all_gather | solution.py:40
  187.3 1.9 copy-start.8
  189.2 1.9 copy-start.6
  195.5 92.3 %collective-permute-start.2 = (f32[2048,256]{1,0:T(8,128)}, f32[2048,256]{1,0:T(8,128)S(1)}, u32[]{:S(2)}, u32[]{:S(2)}) collective-permute-start(f32[2048,256]{1,0:T(8,128)} %get-tuple-element.11), channel_id=1, source_target_pairs={{0,2},{2,4},{4,6},{6,8},{8,10},{10,12},{12,14},{14,0},{1,3},{3,5},... | collective-permute-start | bytes 6291464 | tf_op jit(solution)/shard_map/ppermute | solution.py:12
  197.2 93.0 %collective-permute-start.3 = (f32[2048,256]{1,0:T(8,128)}, f32[2048,256]{1,0:T(8,128)}, u32[]{:S(2)}, u32[]{:S(2)}) collective-permute-start(f32[2048,256]{1,0:T(8,128)} %get-tuple-element.12), channel_id=1, source_target_pairs={{0,14},{2,0},{4,2},{6,4},{8,6},{10,8},{12,10},{14,12},{1,15},{3,1}... | collective-permute-start | bytes 6291464 | tf_op jit(solution)/shard_map/ppermute | solution.py:12
  287.8 1.3 copy-start.10
  292.7 1.3 copy-start.1
  302.1 153.9 %all-gather.15.cloned.1.call-start = ((), (), s32[]{:S(2)}) async-start(), calls=%async_computation.3 | async-start | bytes 3145728 | tf_op jit(solution)/shard_map/all_gather | solution.py:40
  329.7 1.9 copy-start.9
  331.7 1.9 copy-start.2
  337.9 92.3 %collective-permute-start.5 = (f32[2048,256]{1,0:T(8,128)}, f32[2048,256]{1,0:T(8,128)S(1)}, u32[]{:S(2)}, u32[]{:S(2)}) collective-permute-start(f32[2048,256]{1,0:T(8,128)} %get-tuple-element.9), channel_id=1, source_target_pairs={{0,2},{2,4},{4,6},{6,8},{8,10},{10,12},{12,14},{14,0},{1,3},{3,5},... | collective-permute-start | bytes 6291464 | tf_op jit(solution)/shard_map/ppermute | solution.py:12
  339.7 93.0 %collective-permute-start.4 = (f32[2048,256]{1,0:T(8,128)}, f32[2048,256]{1,0:T(8,128)}, u32[]{:S(2)}, u32[]{:S(2)}) collective-permute-start(f32[2048,256]{1,0:T(8,128)} %get-tuple-element.10), channel_id=1, source_target_pairs={{0,14},{2,0},{4,2},{6,4},{8,6},{10,8},{12,10},{14,12},{1,15},{3,1}... | collective-permute-start | bytes 6291464 | tf_op jit(solution)/shard_map/ppermute | solution.py:12
  430.3 1.3 copy-start.11
  435.1 1.3 copy-start.3
  472.4 1.9 copy-start.7
  474.3 1.9 copy-start.4
  480.6 92.3 %collective-permute-start.6 = (f32[2048,256]{1,0:T(8,128)}, f32[2048,256]{1,0:T(8,128)S(1)}, u32[]{:S(2)}, u32[]{:S(2)}) collective-permute-start(f32[2048,256]{1,0:T(8,128)} %get-tuple-element.7), channel_id=1, source_target_pairs={{0,2},{2,4},{4,6},{6,8},{8,10},{10,12},{12,14},{14,0},{1,3},{3,5},... | collective-permute-start | bytes 6291464 | tf_op jit(solution)/shard_map/ppermute | solution.py:12
  482.3 92.8 %collective-permute-start.7 = (f32[2048,256]{1,0:T(8,128)}, f32[2048,256]{1,0:T(8,128)}, u32[]{:S(2)}, u32[]{:S(2)}) collective-permute-start(f32[2048,256]{1,0:T(8,128)} %get-tuple-element.8), channel_id=1, source_target_pairs={{0,14},{2,0},{4,2},{6,4},{8,6},{10,8},{12,10},{14,12},{1,15},{3,1}... | collective-permute-start | bytes 6291464 | tf_op jit(solution)/shard_map/ppermute | solution.py:12
Sparse Core Ops, SparseCore 0:
  17.8 13.2 all-gather.8
  161.1 10.0 all-gather.10
  302.2 11.3 all-gather.12
  444.6 11.3 all-gather.14
